TPU v7x, 32 devices: a whole 2x2x4 slice. The times are simulated.
32 devices in a mesh: vox: 8 (over z, y), frm: 4 (over x, core).
Axes of the slice: x: 2, y: 2, z: 4, core: 2. Of those that a mesh axis runs over, the one named last changes fastest.
Arguments:
- data: bfloat16 [32768, 1024], P('vox', 'frm'), may hold values from -6 to 10.375
- footprints: bfloat16 [64, 4, 512, 128], P('vox'), may hold values from 0 to 1, as said below
- traces: bfloat16 [64, 128, 1024], P('vox', None, 'frm'), may hold values from 0 to 1
- incidence: int32 [64, 4], replicated, may hold values from 0 to 63, as said below
- counts: int32 [64], replicated, may hold values from 1 to 128
Outputs:
- new_traces: bfloat16 [64, 128, 1024], P('vox', None, 'frm')
- new_footprints: bfloat16 [64, 4, 512, 128], P('vox', None, 'frm')
Inputs may be any that keep to these rules, and one draw needn't show every extreme that they name: `incidence`: neuron block j is owned by the device of vox index j // 8. Among the 32 entries of one device's voxel blocks, at most 8 name blocks of one owner, and exactly 8 do for some owner. Over all devices, the blocks of each owner are named exactly 8 * 4 times, and every neuron block is named at least once. `footprints`: every entry is 0 or positive; every neuron column of every tile has a positive entry.
All inputs are finite; a program needn't handle non-finite values.
Results may differ from a plain program's by a relative error of at most 0.0034.
Values may be sent and summed in bfloat16 or wider, within the bound.
A program may use at most 128 MiB of HBM per device.

v0:
```python
import jax
import jax.numpy as jnp
from jax import lax
from jax.sharding import PartitionSpec as P

highest = lax.Precision.HIGHEST


def entry_layout(incidence, owned_blocks, devices):
    per_device = incidence.reshape(devices, -1)
    owners = per_device // owned_blocks
    within = per_device - owners * owned_blocks
    entries = per_device.shape[1]
    position = jnp.arange(entries, dtype=jnp.int32)
    before = position[None, :] < position[:, None]
    same_owner = owners[:, :, None] == owners[:, None, :]
    ranks = jnp.sum((same_owner & before[None, :, :]).astype(jnp.int32), axis=2)
    return (per_device, owners, within, ranks)


def body(data, footprints, traces, incidence, counts):
    devices = lax.axis_size("vox")
    here_index = lax.axis_index("vox")
    frame_parts = lax.axis_size("frm")
    frame_index = lax.axis_index("frm")
    vblocks, touches, block_vox, block_neurons = footprints.shape
    nblocks = traces.shape[0]
    frames = traces.shape[2]
    entries = vblocks * touches
    capacity = 2 * entries // devices
    slot_total = devices * capacity
    rows_quarter = block_vox // frame_parts
    per_device, owners, within, ranks = entry_layout(incidence, nblocks, devices)
    my_block = per_device[here_index]
    my_slot = owners[here_index] * capacity + ranks[here_index]
    from_here = owners == here_index
    sources = jnp.arange(devices, dtype=jnp.int32)[:, None]
    target = jnp.where(from_here, sources * capacity + ranks, slot_total).reshape(-1)
    slot_block = (
        jnp.full((slot_total,), nblocks, jnp.int32).at[target].set(within.reshape(-1), mode="drop")
    )
    neuron = jnp.arange(block_neurons, dtype=jnp.int32)
    own_counts = lax.dynamic_slice_in_dim(counts, here_index * nblocks, nblocks)
    live_own = neuron[None, :] < own_counts[:, None]
    table = jnp.arange(counts.shape[0], dtype=jnp.int32)
    entry_counts = jnp.sum(
        jnp.where(my_block[:, None] == table[None, :], counts[None, :], 0), axis=1
    )
    entry_live = neuron[None, :] < entry_counts[:, None]
    data_blocks = data.reshape(vblocks, block_vox, frames)

    def deliver(own_traces):
        piece = lax.all_gather(own_traces, "vox", axis=0, tiled=True)
        blocks_here = jnp.arange(piece.shape[0], dtype=jnp.int32)
        select = (my_block[:, None] == blocks_here[None, :]).astype(jnp.bfloat16)
        gathered = jnp.einsum("eb,bnf->enf", select, piece, preferred_element_type=jnp.float32)
        return gathered.astype(jnp.bfloat16)

    def residual(entry_traces):
        shaped = entry_traces.reshape(vblocks, touches, block_neurons, frames)
        recon = jnp.einsum("vkxn,vknf->vxf", footprints, shaped, preferred_element_type=jnp.float32)
        return (data_blocks.astype(jnp.float32) - recon).astype(jnp.bfloat16)

    alive = jnp.where(live_own[:, :, None], traces, jnp.zeros((), jnp.bfloat16))
    old_entries = deliver(alive)
    resid = residual(old_entries)
    term = jnp.einsum(
        "vkxn,vxf->vknf", footprints, resid, preferred_element_type=jnp.float32
    ).reshape(entries, block_neurons, frames)
    rowsum = jnp.sum(footprints, axis=(1, 3), dtype=jnp.float32)
    dterm = jnp.einsum(
        "vkxn,vx->vkn", footprints.astype(jnp.float32), rowsum, precision=highest
    ).reshape(entries, block_neurons)
    out_grad = jnp.zeros((slot_total, block_neurons, frames), jnp.float32).at[my_slot].set(term)
    out_denom = jnp.zeros((slot_total, block_neurons), jnp.float32).at[my_slot].set(dterm)
    got_grad, got_denom = (
        lax.all_to_all(out_grad, "vox", split_axis=0, concat_axis=0, tiled=True),
        lax.all_to_all(out_denom, "vox", split_axis=0, concat_axis=0, tiled=True),
    )
    grad = jax.ops.segment_sum(got_grad, slot_block, num_segments=nblocks + 1)[:nblocks]
    denom = jax.ops.segment_sum(got_denom, slot_block, num_segments=nblocks + 1)[:nblocks]
    updated = jnp.maximum(traces.astype(jnp.float32) + grad / denom[:, :, None], 0.0)
    new_traces = jnp.where(live_own[:, :, None], updated, 0.0).astype(jnp.bfloat16)
    new_entries = deliver(new_traces)
    resid_next = residual(new_entries)
    shaped_new = new_entries.reshape(vblocks, touches, block_neurons, frames)
    product = jnp.einsum(
        "vxf,vknf->xvkn", resid_next, shaped_new, preferred_element_type=jnp.float32
    )
    summed = lax.psum_scatter(
        product.reshape(rows_quarter * lax.axis_size("frm"), entries * block_neurons),
        "frm",
        scatter_dimension=0,
        tiled=True,
    )
    fgrad = summed.reshape(rows_quarter, vblocks, touches, block_neurons).transpose(1, 2, 0, 3)
    squares = jnp.sum(jnp.square(new_entries.astype(jnp.float32)), axis=2)
    power = lax.psum(squares, "frm")
    tiles = lax.dynamic_slice_in_dim(footprints, frame_index * rows_quarter, rows_quarter, 2)
    scale = jnp.maximum(power, 1.0).reshape(vblocks, touches, 1, block_neurons)
    keep = entry_live.reshape(vblocks, touches, 1, block_neurons) & (tiles > 0)
    moved = jnp.maximum(tiles.astype(jnp.float32) + fgrad / scale, 0.0)
    new_footprints = jnp.where(keep, moved, 0.0).astype(jnp.bfloat16)
    return (new_traces, new_footprints)


def solution(mesh):
    placed = (P("vox", "frm"), P("vox", None, None, None), P("vox", None, "frm"), P(), P())
    return jax.shard_map(
        body,
        mesh=mesh,
        in_specs=placed,
        out_specs=(P("vox", None, "frm"), P("vox", None, "frm", None)),
        check_vma=False,
    )
```

profile of v0, /device:TPU:0, one launch (start us, length us, event | category | flops | bytes accessed | tf_op | source)
XLA Modules:
  0.0 492.4 jit_solution(8461930699445790062)
XLA Ops:
  7.2 0.7 dynamic_slice.15
  8.0 2.2 broadcast_select_fusion
  10.2 0.8 copy.79
  11.0 0.1 reshape.291
  11.1 0.3 convert_reduce_fusion.1
  11.4 3.0 convert_reduce_fusion
  14.4 0.1 copy-done
  14.5 1.7 fusion.15
  16.2 1.2 scatter_custom_fusion.3
  17.5 7.3 %all-to-all-start.1 = ((f32[8,8,128]{2,1,0:T(8,128)}), f32[8,8,128]{2,1,0:T(8,128)S(1)}, u32[]{:S(2)}, u32[]{:S(2)}) async-start(f32[8,8,128]{2,1,0:T(8,128)} %bitcast.18), calls=%async_computation.1 | async-start | bytes 65536 | tf_op jit(solution)/shard_map/all_to_all | solution.py:78
  24.8 2.9 copy.84
  27.6 60.7 %all-gather.3.cloned.1.call-done = bf16[64,128,256]{2,0,1:T(8,128)(2,1)} async-done(((bf16[8,128,256]{2,0,1:T(8,128)(2,1)}), bf16[64,128,256]{2,0,1:T(8,128)(2,1)}) %all-gather.3.cloned.1.call-update) | async-done | bytes 4194320 | tf_op jit(solution)/shard_map/all_gather | solution.py:53
  88.3 2.9 convolution_convert_fusion.1
  91.3 3.1 copy.102
  94.4 9.7 %fusion.4 = f32[8,256,4,128]{3,1,2,0:T(8,128)} fusion(bf16[8,4,512,128]{3,2,1,0:T(8,128)(2,1)} %param.6, f32[8,512,256]{1,2,0:T(8,128)} %copy.84, bf16[8,4,128,256]{2,3,1,0:T(8,128)(2,1)} %bitcast.86), kind=kOutput, calls=%fused_computation.13 | convolution fusion | flops 2149580800 | bytes 14680064 | tf_op jit(solution)/shard_map/vkxn,vxf->vknf/dot_general | solution.py:67
  104.1 5.6 %copy.85 = f32[32,128,256]{2,1,0:T(8,128)} copy(f32[32,128,256]{1,2,0:T(8,128)} %bitcast.85) | data formatting | bytes 8388608 | tf_op jit(solution)/shard_map/reshape | solution.py:69
  109.7 4.2 broadcast_in_dim.82
  114.0 8.3 %scatter_fusion = f32[64,128,256]{2,1,0:T(8,128)} fusion(f32[64,128,256]{2,1,0:T(8,128)} %broadcast_in_dim.82, s32[32]{0:T(128)S(1)} %fusion.30, f32[32,128,256]{2,1,0:T(8,128)} %copy.85), kind=kCustom, calls=%fused_computation.1 | custom fusion | bytes 12583040 | tf_op jit(solution)/shard_map/scatter | solution.py:74
  122.2 5.0 %all-to-all-start = ((f32[64,128,256]{2,1,0:T(8,128)}), f32[64,128,256]{2,1,0:T(8,128)}, u32[]{:S(2)}, u32[]{:S(2)}) async-start(f32[64,128,256]{2,1,0:T(8,128)} %scatter_fusion), calls=%async_computation | async-start | bytes 16777216 | tf_op jit(solution)/shard_map/all_to_all | solution.py:77
  127.3 0.0 all-gather.5.cloned.1.call-start
  127.3 0.1 reshape.290
  127.5 0.1 reshape.292
  127.6 0.1 broadcast_add_fusion
  127.6 0.1 add.100
  127.8 1.4 scatter_custom_fusion
  129.2 1.0 scatter_custom_fusion.4
  130.2 0.1 copy.87
  130.3 179.6 %all-to-all-done = f32[64,128,256]{2,1,0:T(8,128)} async-done(((f32[64,128,256]{2,1,0:T(8,128)}), f32[64,128,256]{2,1,0:T(8,128)}, u32[]{:S(2)}, u32[]{:S(2)}) %all-to-all-start) | async-done | bytes 8388640 | tf_op jit(solution)/shard_map/all_to_all | solution.py:77
  309.9 0.1 broadcast_in_dim.46
  310.0 12.4 %scatter_fusion.1 = f32[9,128,256]{2,1,0:T(8,128)S(1)} fusion(f32[9,128,256]{2,1,0:T(8,128)S(1)} %broadcast_in_dim.46, s32[64]{0:T(128)S(1)} %scatter_custom_fusion, f32[64,128,256]{2,1,0:T(8,128)} %all-to-all-done), kind=kCustom, calls=%fused_computation.2 | custom fusion | flops 2097152 | bytes 25166080 | tf_op jit(solution)/shard_map/scatter-add | solution.py:80
  322.4 0.1 slice.8
  322.5 1.8 fusion.12
  324.4 73.8 %all-gather.5.cloned.1.call-done = bf16[64,128,256]{2,0,1:T(8,128)(2,1)} async-done(((bf16[8,128,256]{2,0,1:T(8,128)(2,1)}), bf16[64,128,256]{2,0,1:T(8,128)(2,1)}) %all-gather.5.cloned.1.call-update) | async-done | bytes 4194320 | tf_op jit(solution)/shard_map/all_gather | solution.py:53
  398.2 3.1 multiply_reduce_fusion
  401.4 1.2 copy.107
  402.6 9.2 %fusion.2 = f32[8,4,128,512]{3,2,1,0:T(8,128)} fusion(bf16[8,4,128,256]{3,2,1,0:T(8,128)(2,1)S(1)} %bitcast.84, f32[8,512,256]{1,2,0:T(8,128)} %copy.84, bf16[8,4,512,128]{3,2,1,0:T(8,128)(2,1)} %param.6), kind=kOutput, calls=%fused_computation.11 | convolution fusion | flops 2149580800 | bytes 18874368 | tf_op jit(solution)/shard_map/vxf,vknf->xvkn/dot_general | solution.py:87
  411.8 0.6 copy-done.4
  412.4 0.2 select_reduce_fusion
  412.6 0.1 lt.97
  412.7 1.3 constant_dynamic-slice_fusion
  414.0 0.7 copy.106
  414.6 0.1 iota_compare_fusion.1
  414.7 0.9 copy.94
  415.6 0.1 copy.93
  415.7 10.2 %psum.7 = f32[32,128]{1,0:T(8,128)S(1)} all-reduce(f32[32,128]{1,0:T(8,128)S(1)} %copy.93), channel_id=1, replica_groups=mesh['vox'=8,'frm'=4] {'frm'}, use_global_device_ids=true, to_apply=%region_10.11 | all-reduce | flops 4096 | bytes 32768 | tf_op jit(solution)/shard_map/psum | solution.py:98
  425.9 55.4 %reduce-scatter.2.cloned.1.call-done = f32[128,4096]{0,1:T(8,128)} async-done(((f32[512,4096]{0,1:T(8,128)}), f32[128,4096]{0,1:T(8,128)}) %reduce-scatter.2.cloned.1.call-update) | async-done | bytes 2097168 | tf_op jit(solution)/shard_map/reduce_scatter | solution.py:90
  481.3 3.2 fusion.8
  484.5 1.3 copy.95
  (24 shorter events, 0.2 us)
Async XLA Ops:
  7.2 81.2 %all-gather.3.cloned.1.call-start = ((), (), s32[]{:S(2)}) async-start(), calls=%async_computation.3 | async-start | bytes 4718592 | tf_op jit(solution)/shard_map/all_gather | solution.py:53
  11.0 3.5 copy-start
  11.4 13.4 %copy-start.2 = (bf16[4096,256]{1,0:T(8,128)(2,1)S(1)}, bf16[4096,256]{1,0:T(8,128)(2,1)}, u32[]{:S(2)}) copy-start(bf16[4096,256]{1,0:T(8,128)(2,1)} %param.5) | copy-start | bytes 6291460
  17.5 104.8 %all-to-all-start.1 = ((f32[8,8,128]{2,1,0:T(8,128)}), f32[8,8,128]{2,1,0:T(8,128)S(1)}, u32[]{:S(2)}, u32[]{:S(2)}) async-start(f32[8,8,128]{2,1,0:T(8,128)} %bitcast.18), calls=%async_computation.1 | async-start | bytes 65536 | tf_op jit(solution)/shard_map/all_to_all | solution.py:78
  122.2 187.7 %all-to-all-start = ((f32[64,128,256]{2,1,0:T(8,128)}), f32[64,128,256]{2,1,0:T(8,128)}, u32[]{:S(2)}, u32[]{:S(2)}) async-start(f32[64,128,256]{2,1,0:T(8,128)} %scatter_fusion), calls=%async_computation | async-start | bytes 16777216 | tf_op jit(solution)/shard_map/all_to_all | solution.py:77
  127.3 270.9 %all-gather.5.cloned.1.call-start = ((), (), s32[]{:S(2)}) async-start(), calls=%async_computation.4 | async-start | bytes 4718592 | tf_op jit(solution)/shard_map/all_gather | solution.py:53
  310.0 12.5 %copy-start.3 = (bf16[8,128,256]{2,1,0:T(8,128)(2,1)S(1)}, bf16[8,128,256]{2,1,0:T(8,128)(2,1)}, u32[]{:S(2)}) copy-start(bf16[8,128,256]{2,1,0:T(8,128)(2,1)} %param.7) | copy-start | bytes 1572868
  324.3 157.0 %reduce-scatter.2.cloned.1.call-start = ((), (), s32[]{:S(2)}) async-start(), calls=%async_computation.5 | async-start | bytes 10485760 | tf_op jit(solution)/shard_map/reduce_scatter | solution.py:90
  411.7 0.7 copy-start.4
  412.4 2.3 copy-start.1
Sparse Core Ops, SparseCore 0:
  10.6 77.7 all-gather.2
  324.5 73.7 all-gather.4
  411.9 69.3 reduce-scatter.1
where the time goes:
time: 493 us; the launch traced here: 492 us
  waiting for transfers between devices  370 us (75%)
  local copies, waits for them, and re-layouts  35.1 us (7%)
  matrix products  26.8 us (5%)
  other arithmetic  24.3 us (5%)
  between operations  13.9 us (3%)
  starting transfers between devices  12.5 us (3%)
  blocking collectives  10.2 us (2%)
    all_to_all x1, waiting for transfers between devices, body(): lax.all_to_all(out_grad, 'vox', split_axis=0, concat_axis=0, tiled=True)  180 us
    all_gather x2, waiting for transfers between devices, deliver(): piece = lax.all_gather(own_traces, 'vox', axis=0, tiled=True)  135 us
    reduce_scatter x1, waiting for transfers between devices, body(): lax.psum_scatter(product.reshape(rows_quarter * lax.axis_size('frm'), ent...  55.4 us
    scatter-add x1, other arithmetic, body(): jax.ops.segment_sum(got_grad, slot_block, num_segments=nblocks + 1)  12.4 us
    psum x1, blocking collectives, body(): power = lax.psum(squares, 'frm')  10.2 us
  transfers between devices with their start and end apart: 5, of which 4 were waited for; matrix products, arithmetic and copies ran while one was open for 10% of the time, Pallas kernels for 0%

commit v1 on v0

--- a/solution.py
+++ b/solution.py
@@ -1,7 +1,461 @@
+import functools
 import jax
 import jax.numpy as jnp
 from jax import lax
+from jax.experimental import pallas as pl
+from jax.experimental.pallas import tpu as pltpu
 from jax.sharding import PartitionSpec as P
+
+VMEM = pltpu.VMEM
+NT = (((1,), (1,)), ((), ()))
+TN = (((0,), (0,)), ((), ()))
+
+
+def matmul(a, b, dims=(((1,), (0,)), ((), ()))):
+    return lax.dot_general(a, b, dims, preferred_element_type=jnp.float32)
+
+
+def split_two(value):
+    high = value.astype(jnp.bfloat16)
+    return high, (value - high.astype(jnp.float32)).astype(jnp.bfloat16)
+
+
+def ring_position(index, n):
+    odd = lax.rem(index, 2)
+    half = index // 2
+    return (1 - odd) * half + odd * (n - 1 - half)
+
+
+def ring_index(position, n):
+    q = lax.rem(position + 2 * n, n)
+    upper = q // (n // 2)
+    return (1 - upper) * 2 * q + upper * (2 * n - 1 - 2 * q)
+
+
+def greet(peers):
+    barrier = pltpu.get_barrier_semaphore()
+    for peer in peers:
+        pl.semaphore_signal(
+            barrier, inc=1, device_id=peer, device_id_type=pl.DeviceIdType.MESH
+        )
+    pl.semaphore_wait(barrier, len(peers))
+
+
+class Ring:
+    def __init__(self, n, nb, subs):
+        self.n, self.nb, self.subs = n, nb, subs
+        self.hops = n // 2
+        self.step = nb // subs
+        self.me = lax.axis_index("vox")
+        self.pos = ring_position(self.me, n)
+        self.next = (ring_index(self.pos + 1, n), ring_index(self.pos - 1, n))
+
+    def owner(self, way, distance):
+        return ring_index(self.pos + (distance if way == 0 else -distance), self.n)
+
+    def rows(self, owner, sub):
+        return pl.ds(owner * self.nb + sub * self.step, self.step)
+
+    def far_part(self, way, sub):
+        return (sub < self.subs // 2) == (way == 0)
+
+    def copy(self, src, dst, send, recv, way):
+        return pltpu.make_async_remote_copy(
+            src_ref=src,
+            dst_ref=dst,
+            send_sem=send,
+            recv_sem=recv,
+            device_id={"vox": self.next[way]},
+            device_id_type=pl.DeviceIdType.MESH,
+        )
+
+
+def gather_copy(ring, own, full, send, recv, way, hop, sub):
+    rows = ring.rows(ring.owner(way, -hop), sub)
+    src = own.at[pl.ds(sub * ring.step, ring.step)] if hop == 0 else full.at[rows]
+    return ring.copy(src, full.at[rows], send.at[way, hop, sub], recv.at[way, hop, sub], way)
+
+
+def gather_rest(ring, own, full, send, recv):
+    copy = functools.partial(gather_copy, ring, own, full, send, recv)
+    last = ring.hops - 1
+
+    def used(way, hop, sub):
+        return hop < last or ring.far_part(way, sub)
+
+    for hop in range(1, ring.hops + 1):
+        for sub in range(ring.subs):
+            for way in range(2):
+                if used(way, hop - 1, sub):
+                    copy(way, hop - 1, sub).wait_recv()
+                    if hop <= last and used(way, hop, sub):
+                        copy(way, hop, sub).start()
+    for hop in range(ring.hops):
+        for sub in range(ring.subs):
+            for way in range(2):
+                if used(way, hop, sub):
+                    copy(way, hop, sub).wait_send()
+
+
+def gather_kernel(n, subs, own, full, send, recv):
+    nb = own.shape[0]
+    ring = Ring(n, nb, subs)
+    greet([{"vox": peer} for peer in ring.next])
+    for sub in range(subs):
+        for way in range(2):
+            gather_copy(ring, own, full, send, recv, way, 0, sub).start()
+    full[pl.ds(ring.me * nb, nb)] = own[...]
+    gather_rest(ring, own, full, send, recv)
+
+
+def gather_traces(traces, n, subs):
+    nb, bn, t = traces.shape
+    return pl.pallas_call(
+        functools.partial(gather_kernel, n, subs),
+        out_shape=jax.ShapeDtypeStruct((n * nb, bn, t), jnp.bfloat16),
+        in_specs=[pl.BlockSpec(memory_space=VMEM)],
+        out_specs=pl.BlockSpec(memory_space=VMEM),
+        scratch_shapes=[
+            pltpu.SemaphoreType.DMA((2, n // 2, subs)),
+            pltpu.SemaphoreType.DMA((2, n // 2, subs)),
+        ],
+        compiler_params=pltpu.CompilerParams(collective_id=0, has_side_effects=True),
+        name="gather_traces",
+    )(traces)
+
+
+def recon_of(foot, entries):
+    total = None
+    for tile, entry in zip(foot, entries):
+        part = matmul(tile, entry)
+        total = part if total is None else total + part
+    return total
+
+
+def term_kernel(block_ref, counts_ref, foot_ref, data_ref, full_ref, part_ref, denom_ref, total):
+    step = pl.program_id(0)
+    touches, _, bn = foot_ref.shape[1:]
+
+    @pl.when(step == 0)
+    def _():
+        total[...] = jnp.zeros_like(total)
+        denom_ref[...] = jnp.zeros_like(denom_ref)
+
+    foot = [foot_ref[0, k] for k in range(touches)]
+    named = [block_ref[step, k] for k in range(touches)]
+    neuron = lax.broadcasted_iota(jnp.int32, full_ref.shape[1:], 0)
+    entries = [
+        jnp.where(neuron < counts_ref[j], full_ref[j], jnp.zeros((), jnp.bfloat16)) for j in named
+    ]
+    resid = (data_ref[...].astype(jnp.float32) - recon_of(foot, entries)).astype(jnp.bfloat16)
+    ones = jnp.ones((8, bn), jnp.bfloat16)
+    rowsum = None
+    for tile in foot:
+        part = matmul(ones, tile, NT)
+        rowsum = part if rowsum is None else rowsum + part
+    high, low = split_two(rowsum)
+    for k, j in enumerate(named):
+        total[j] += matmul(foot[k], resid, TN)
+        dterm = matmul(high, foot[k]) + matmul(low, foot[k])
+        denom_ref[pl.ds(j, 1), :] += dterm[:1]
+
+    @pl.when(step == pl.num_programs(0) - 1)
+    def _():
+        part_ref[...] = total[...].astype(jnp.bfloat16)
+
+
+def terms(my_block, counts, footprints, data, full):
+    vblocks, touches, bv, bn = footprints.shape
+    blocks, _, t = full.shape
+    return pl.pallas_call(
+        term_kernel,
+        out_shape=(
+            jax.ShapeDtypeStruct(full.shape, jnp.bfloat16),
+            jax.ShapeDtypeStruct((blocks, bn), jnp.float32),
+        ),
+        grid_spec=pltpu.PrefetchScalarGridSpec(
+            num_scalar_prefetch=2,
+            grid=(vblocks,),
+            in_specs=[
+                pl.BlockSpec((1, touches, bv, bn), lambda i, *_: (i, 0, 0, 0)),
+                pl.BlockSpec((bv, t), lambda i, *_: (i, 0)),
+                pl.BlockSpec((blocks, bn, t), lambda i, *_: (0, 0, 0)),
+            ],
+            out_specs=(
+                pl.BlockSpec((blocks, bn, t), lambda i, *_: (0, 0, 0)),
+                pl.BlockSpec((blocks, bn), lambda i, *_: (0, 0)),
+            ),
+            scratch_shapes=[pltpu.VMEM((blocks, bn, t), jnp.float32)],
+        ),
+        name="terms",
+    )(my_block, counts, footprints, data, full)
+
+
+def update_kernel(
+    n, subs, part, denom, own, live, new, full, got, out, dgot, send, recv, dsend, drecv, asend, arecv
+):
+    nb = own.shape[0]
+    ring = Ring(n, nb, subs)
+    hops = ring.hops
+    peers = [lax.rem(ring.me + k, n) for k in range(1, n)]
+    greet([{"vox": peer} for peer in peers])
+
+    def used(way, hop, sub):
+        return hop > 0 or ring.far_part(way, sub)
+
+    def piece(sub):
+        return pl.ds(sub * ring.step, ring.step)
+
+    def copy(way, hop, sub):
+        rows = ring.rows(ring.owner(way, hops - hop), sub)
+        first = hop == 0 or not used(way, hop - 1, sub)
+        src = part.at[rows] if first else out.at[way, hop, piece(sub)]
+        return ring.copy(
+            src, got.at[way, hop, piece(sub)], send.at[way, hop, sub], recv.at[way, hop, sub], way
+        )
+
+    def dcopy(k):
+        peer = peers[k - 1]
+        return pltpu.make_async_remote_copy(
+            src_ref=denom.at[peer],
+            dst_ref=dgot.at[k - 1],
+            send_sem=dsend.at[k - 1],
+            recv_sem=drecv.at[k - 1],
+            device_id={"vox": peer},
+            device_id_type=pl.DeviceIdType.MESH,
+        )
+
+    for hop in range(hops):
+        for sub in range(subs):
+            for way in range(2):
+                if not used(way, hop, sub):
+                    continue
+                if hop > 0 and used(way, hop - 1, sub):
+                    copy(way, hop - 1, sub).wait_recv()
+                    rows = ring.rows(ring.owner(way, hops - hop), sub)
+                    summed = got[way, hop - 1, piece(sub)].astype(jnp.float32) + part[rows].astype(
+                        jnp.float32
+                    )
+                    out[way, hop, piece(sub)] = summed.astype(jnp.bfloat16)
+                copy(way, hop, sub).start()
+        if hop == 0:
+            for k in range(1, n):
+                dcopy(k).start()
+    total = denom[ring.me]
+    for k in range(1, n):
+        dcopy(k).wait_recv()
+        total = total + dgot[k - 1]
+    columns = jnp.transpose(total)
+    alive = jnp.transpose(live[...])
+    for sub in range(subs):
+        for way in range(2):
+            copy(way, hops - 1, sub).wait_recv()
+        rows = ring.rows(ring.me, sub)
+        grad = part[rows].astype(jnp.float32)
+        for way in range(2):
+            grad = grad + got[way, hops - 1, piece(sub)].astype(jnp.float32)
+        for b in range(ring.step):
+            j = sub * ring.step + b
+            moved = own[j].astype(jnp.float32) + grad[b] / columns[:, j : j + 1]
+            moved = jnp.where(alive[:, j : j + 1] > 0, jnp.maximum(moved, 0.0), 0.0)
+            new[j] = moved.astype(jnp.bfloat16)
+        for way in range(2):
+            gather_copy(ring, new, full, asend, arecv, way, 0, sub).start()
+    full[pl.ds(ring.me * nb, nb)] = new[...]
+    gather_rest(ring, new, full, asend, arecv)
+    for hop in range(hops):
+        for sub in range(subs):
+            for way in range(2):
+                if used(way, hop, sub):
+                    copy(way, hop, sub).wait_send()
+    for k in range(1, n):
+        dcopy(k).wait_send()
+
+
+def update_traces(part, denom, traces, live, n, subs):
+    nb, bn, t = traces.shape
+    hops = n // 2
+    return pl.pallas_call(
+        functools.partial(update_kernel, n, subs),
+        out_shape=(
+            jax.ShapeDtypeStruct(traces.shape, jnp.bfloat16),
+            jax.ShapeDtypeStruct(part.shape, jnp.bfloat16),
+        ),
+        in_specs=[pl.BlockSpec(memory_space=VMEM)] * 4,
+        out_specs=(pl.BlockSpec(memory_space=VMEM),) * 2,
+        scratch_shapes=[
+            pltpu.VMEM((2, hops, nb, bn, t), jnp.bfloat16),
+            pltpu.VMEM((2, hops, nb, bn, t), jnp.bfloat16),
+            pltpu.VMEM((n - 1, nb, bn), jnp.float32),
+            pltpu.SemaphoreType.DMA((2, hops, subs)),
+            pltpu.SemaphoreType.DMA((2, hops, subs)),
+            pltpu.SemaphoreType.DMA((n - 1,)),
+            pltpu.SemaphoreType.DMA((n - 1,)),
+            pltpu.SemaphoreType.DMA((2, hops, subs)),
+            pltpu.SemaphoreType.DMA((2, hops, subs)),
+        ],
+        compiler_params=pltpu.CompilerParams(collective_id=1, has_side_effects=True),
+        name="update_traces",
+    )(part, denom.reshape(n, nb, bn), traces, live)
+
+
+def foot_kernel(block_ref, foot_ref, data_ref, full_ref, grad_ref, power_ref):
+    step = pl.program_id(0)
+    touches, _, bn = foot_ref.shape[1:]
+    foot = [foot_ref[0, k] for k in range(touches)]
+    entries = [full_ref[block_ref[step, k]] for k in range(touches)]
+    resid = (data_ref[...].astype(jnp.float32) - recon_of(foot, entries)).astype(jnp.bfloat16)
+    ones = jnp.ones((8, full_ref.shape[2]), jnp.bfloat16)
+    for k, entry in enumerate(entries):
+        grad_ref[0, k] = matmul(resid, entry, NT).astype(jnp.bfloat16)
+        wide = entry.astype(jnp.float32)
+        high, low = split_two(wide * wide)
+        squares = matmul(ones, high, NT) + matmul(ones, low, NT)
+        power_ref[0, k : k + 1, :] = squares[:1]
+
+
+def foot_terms(my_block, footprints, data, full):
+    vblocks, touches, bv, bn = footprints.shape
+    blocks, _, t = full.shape
+    return pl.pallas_call(
+        foot_kernel,
+        out_shape=(
+            jax.ShapeDtypeStruct(footprints.shape, jnp.bfloat16),
+            jax.ShapeDtypeStruct((vblocks, touches, bn), jnp.float32),
+        ),
+        grid_spec=pltpu.PrefetchScalarGridSpec(
+            num_scalar_prefetch=1,
+            grid=(vblocks,),
+            in_specs=[
+                pl.BlockSpec((1, touches, bv, bn), lambda i, *_: (i, 0, 0, 0)),
+                pl.BlockSpec((bv, t), lambda i, *_: (i, 0)),
+                pl.BlockSpec((blocks, bn, t), lambda i, *_: (0, 0, 0)),
+            ],
+            out_specs=(
+                pl.BlockSpec((1, touches, bv, bn), lambda i, *_: (i, 0, 0, 0)),
+                pl.BlockSpec((1, touches, bn), lambda i, *_: (i, 0, 0)),
+            ),
+        ),
+        name="foot_terms",
+    )(my_block, footprints, data, full)
+
+
+def spread_kernel(parts, grad, power, tiles, live, new, pair, cross, out, pgot, psem, csem, wsem):
+    vblocks, touches, bv, bn = grad.shape
+    rows = bv // parts
+    me = lax.axis_index("frm")
+    line, core = me // 2, lax.rem(me, 2)
+    mate = line * 2 + 1 - core
+    far = (1 - line) * 2 + core
+    others = [lax.rem(me + k, parts) for k in range(1, parts)]
+    greet([{"frm": peer} for peer in others])
+
+    def remote(src, dst, send, recv, peer):
+        return pltpu.make_async_remote_copy(
+            src_ref=src,
+            dst_ref=dst,
+            send_sem=send,
+            recv_sem=recv,
+            device_id={"frm": peer},
+            device_id_type=pl.DeviceIdType.MESH,
+        )
+
+    def quarter(index):
+        return pl.ds(index * rows, rows)
+
+    def to_mate(v, slot):
+        target = (line if slot == 1 else 1 - line) * 2 + 1 - core
+        return remote(
+            grad.at[v, :, quarter(target)],
+            pair.at[slot, v],
+            psem.at[0, slot, v],
+            psem.at[1, slot, v],
+            mate,
+        )
+
+    def to_far(v):
+        return remote(out.at[v], cross.at[v], csem.at[0, v], csem.at[1, v], far)
+
+    def to_other(k):
+        return remote(power, pgot.at[k - 1], wsem.at[0, k - 1], wsem.at[1, k - 1], others[k - 1])
+
+    for v in range(vblocks):
+        to_mate(v, 0).start()
+    for k in range(1, parts):
+        to_other(k).start()
+    for v in range(vblocks):
+        to_mate(v, 1).start()
+    for v in range(vblocks):
+        to_mate(v, 0).wait_recv()
+        summed = grad[v, :, quarter(far)].astype(jnp.float32) + pair[0, v].astype(jnp.float32)
+        out[v] = summed.astype(jnp.bfloat16)
+        to_far(v).start()
+    total = power[...]
+    for k in range(1, parts):
+        to_other(k).wait_recv()
+        total = total + pgot[k - 1]
+    scale = 1.0 / jnp.maximum(total, 1.0)
+    for v in range(vblocks):
+        to_mate(v, 1).wait_recv()
+        to_far(v).wait_recv()
+        for k in range(touches):
+            moved = grad[v, k, quarter(me)].astype(jnp.float32) + pair[1, v, k].astype(jnp.float32)
+            moved = moved + cross[v, k].astype(jnp.float32)
+            old = tiles[v, k].astype(jnp.float32)
+            moved = jnp.maximum(old + moved * scale[v, k : k + 1], 0.0)
+            keep = (old > 0) & (live[v, k : k + 1] > 0)
+            new[v, k] = jnp.where(keep, moved, 0.0).astype(jnp.bfloat16)
+    for v in range(vblocks):
+        to_mate(v, 0).wait_send()
+        to_mate(v, 1).wait_send()
+        to_far(v).wait_send()
+    for k in range(1, parts):
+        to_other(k).wait_send()
+
+
+def spread_footprints(grad, power, tiles, live, parts):
+    vblocks, touches, bv, bn = grad.shape
+    shape = (vblocks, touches, bv // parts, bn)
+    return pl.pallas_call(
+        functools.partial(spread_kernel, parts),
+        out_shape=jax.ShapeDtypeStruct(shape, jnp.bfloat16),
+        in_specs=[pl.BlockSpec(memory_space=VMEM)] * 4,
+        out_specs=pl.BlockSpec(memory_space=VMEM),
+        scratch_shapes=[
+            pltpu.VMEM((2,) + shape, jnp.bfloat16),
+            pltpu.VMEM(shape, jnp.bfloat16),
+            pltpu.VMEM(shape, jnp.bfloat16),
+            pltpu.VMEM((parts - 1,) + power.shape, jnp.float32),
+            pltpu.SemaphoreType.DMA((2, 2, vblocks)),
+            pltpu.SemaphoreType.DMA((2, vblocks)),
+            pltpu.SemaphoreType.DMA((2, parts - 1)),
+        ],
+        compiler_params=pltpu.CompilerParams(collective_id=2, has_side_effects=True),
+        name="spread_footprints",
+    )(grad, power, tiles, live)
+
+
+def ring_body(data, footprints, traces, incidence, counts):
+    n = lax.axis_size("vox")
+    here = lax.axis_index("vox")
+    parts = lax.axis_size("frm")
+    vblocks, touches, bv, bn = footprints.shape
+    nb = traces.shape[0]
+    subs = 4 if nb % 4 == 0 else 2
+    my_block = lax.dynamic_slice_in_dim(incidence, here * vblocks, vblocks)
+    neuron = jnp.arange(bn, dtype=jnp.int32)
+    own_counts = lax.dynamic_slice_in_dim(counts, here * nb, nb)
+    live_own = (neuron[None, :] < own_counts[:, None]).astype(jnp.float32)
+    entry_live = (neuron < counts[my_block][:, :, None]).astype(jnp.float32)
+    rows = bv // parts
+    tiles = lax.dynamic_slice_in_dim(footprints, lax.axis_index("frm") * rows, rows, 2)
+    full = gather_traces(traces, n, subs)
+    part, denom = terms(my_block, counts, footprints, data, full)
+    new_traces, new_full = update_traces(part, denom, traces, live_own, n, subs)
+    grad, power = foot_terms(my_block, footprints, data, new_full)
+    new_footprints = spread_footprints(grad, power, tiles, entry_live, parts)
+    return (new_traces, new_footprints)
+
 
 highest = lax.Precision.HIGHEST
 
@@ -18,7 +472,7 @@
     return (per_device, owners, within, ranks)
 
 
-def body(data, footprints, traces, incidence, counts):
+def slot_body(data, footprints, traces, incidence, counts):
     devices = lax.axis_size("vox")
     here_index = lax.axis_index("vox")
     frame_parts = lax.axis_size("frm")
@@ -104,6 +558,14 @@
     return (new_traces, new_footprints)
 
 
+def body(data, footprints, traces, incidence, counts):
+    devices = lax.axis_size("vox")
+    entries = footprints.shape[0] * footprints.shape[1]
+    dense = 2 * entries // devices >= traces.shape[0] and lax.axis_size("frm") == 4
+    chosen = ring_body if dense else slot_body
+    return chosen(data, footprints, traces, incidence, counts)
+
+
 def solution(mesh):
     placed = (P("vox", "frm"), P("vox", None, None, None), P("vox", None, "frm"), P(), P())
     return jax.shard_map(

time: 493 us -> 209 us (0.42)
  waiting for transfers between devices: 370 us -> 0 us
  Pallas kernels: 0 us -> 199 us
  local copies, waits for them, and re-layouts: 35.1 us -> 7.84 us
  matrix products: 26.8 us -> 0 us
  other arithmetic: 24.3 us -> 1.37 us
  between operations: 13.9 us -> 0.7 us
  starting transfers between devices: 12.5 us -> 0 us
  blocking collectives: 10.2 us -> 0 us
    pallas_call x0 -> x5, Pallas kernels: none -> 199 us  [the longest x1 89.3 us: update_traces(): pl.pallas_call(functools.partial(update_kernel, n, subs), out_shape=(jax....]
    all_to_all x2 -> x0, waiting for transfers between devices: 180 us -> none  [the longest x1 180 us: body(): lax.all_to_all(out_grad, 'vox', split_axis=0, concat_axis=0, tiled=True)]
    all_gather x2 -> x0, waiting for transfers between devices: 135 us -> none  [deliver(): piece = lax.all_gather(own_traces, 'vox', axis=0, tiled=True)]
    reduce_scatter x1 -> x0, waiting for transfers between devices: 55.4 us -> none  [body(): lax.psum_scatter(product.reshape(rows_quarter * lax.axis_size('frm'), ent...]
    dot_general x5 -> x0, matrix products: 26.8 us -> none  [the longest x1 9.75 us: body(): jnp.einsum('vkxn,vxf->vknf', footprints, resid, preferred_element_type=jn...]
    scatter-add x2 -> x0, other arithmetic: 13.4 us -> none  [the longest x1 12.4 us: body(): jax.ops.segment_sum(got_grad, slot_block, num_segments=nblocks + 1)]
    all_to_all x2 -> x0, starting transfers between devices: 12.4 us -> none  [the longest x1 7.31 us: body(): lax.all_to_all(out_denom, 'vox', split_axis=0, concat_axis=0, tiled=True)]
    scatter x3 -> x0, local copies, waits for them, and re-layouts: 10.9 us -> none  [the longest x1 8.29 us: body(): jnp.zeros((slot_total, block_neurons, frames), jnp.float32).at[my_slot]]
  transfers between devices with their start and end apart: 5 -> 0, of which waited for: 4 -> 0; matrix products, arithmetic and copies ran while one was open for 10% -> 0% of each run, Pallas kernels for 0% -> 0%
where the time goes in v1:
time: 209 us
  Pallas kernels  199 us (95%)
  local copies, waits for them, and re-layouts  7.84 us (4%)
    pallas_call x1, Pallas kernels, update_traces(): pl.pallas_call(functools.partial(update_kernel, n, subs), out_shape=(jax....  89.3 us
    pallas_call x1, Pallas kernels, gather_traces(): pl.pallas_call(functools.partial(gather_kernel, n, subs), out_shape=jax.S...  48 us
    pallas_call x1, Pallas kernels, spread_footprints(): pl.pallas_call(functools.partial(spread_kernel, parts), out_shape=jax.Sha...  30.8 us
    pallas_call x1, Pallas kernels, terms(): pl.pallas_call(term_kernel, out_shape=(jax.ShapeDtypeStruct(full.shape, j...  16 us
    pallas_call x1, Pallas kernels, foot_terms(): pl.pallas_call(foot_kernel, out_shape=(jax.ShapeDtypeStruct(footprints.sh...  14.9 us
    unnamed x11, local copies, waits for them, and re-layouts  4.47 us

profile of v1, /device:TPU:0, one launch (start us, length us, event | category | flops | bytes accessed | tf_op | source)
XLA Modules:
  0.0 208.9 jit_solution(4767926045402858838)
XLA Ops:
  0.6 0.0 copy-start
  0.7 0.7 copy-done
  1.3 0.1 constant_dynamic-slice_fusion.1
  1.4 0.7 copy.9.block_ref
  2.1 48.0 %gather_traces.1.full_ref = bf16[64,128,256]{2,1,0:T(8,128)(2,1)} custom-call(bf16[8,128,256]{2,1,0:T(8,128)(2,1)} %own.3), custom_call_target="tpu_custom_call" | custom-call | tf_op jit(solution)/shard_map/gather_traces/pallas_call | solution.py:113
  50.1 0.0 copy-start.1
  50.1 16.0 %terms.1 = (bf16[64,128,256]{2,1,0:T(8,128)(2,1)}, f32[64,128]{1,0:T(8,128)}) custom-call(s32[8,4]{1,0:T(8,128)} %copy.9.block_ref, s32[64]{0:T(128)} %counts_ref.1, bf16[8,4,512,128]{3,2,1,0:T(8,128)(2,1)} %foot_ref.3, bf16[4096,256]{1,0:T(8,128)(2,1)} %data_ref.3, bf16[64,128,256]{2,1,0:T(8,128)(2,1)} %gather_traces.1.full_ref), custom_call_target="tpu_custom_call" | custom-call | tf_op jit(solution)/shard_map/terms/pallas_call | solution.py:170
  66.1 0.0 copy-done.1
  66.1 0.1 dynamic_slice.10
  66.1 0.7 fusion.1.live
  66.8 89.3 %update_traces.1 = (bf16[8,128,256]{2,1,0:T(8,128)(2,1)}, bf16[64,128,256]{2,1,0:T(8,128)(2,1)}) custom-call(bf16[64,128,256]{2,1,0:T(8,128)(2,1)} %get-tuple-element.8.part, f32[8,8,128]{2,1,0:T(8,128)} %bitcast.1, bf16[8,128,256]{2,1,0:T(8,128)(2,1)} %own.3, f32[8,128]{1,0:T(8,128)} %fusion.1.live), custom_call_target="tpu_custom_call" | custom-call | tf_op jit(solution)/shard_map/update_traces/pallas_call | solution.py:278
  156.1 0.0 copy-start.3
  156.1 14.9 %foot_terms.1 = (bf16[8,4,512,128]{3,2,1,0:T(8,128)(2,1)}, f32[8,4,128]{2,1,0:T(4,128)}) custom-call(s32[8,4]{1,0:T(8,128)} %copy.9.block_ref, bf16[8,4,512,128]{3,2,1,0:T(8,128)(2,1)} %foot_ref.3, bf16[4096,256]{1,0:T(8,128)(2,1)} %data_ref.3, bf16[64,128,256]{2,1,0:T(8,128)(2,1)} %get-tuple-element.11.full_ref), custom_call_target="tpu_custom_call" | custom-call | tf_op jit(solution)/shard_map/foot_terms/pallas_call | solution.py:320
  171.0 0.0 copy-done.3
  171.0 0.1 reshape.12
  171.1 0.7 gather_fusion
  171.8 0.1 reshape.11
  171.8 0.7 fusion.live
  172.5 0.0 copy-start.2
  172.5 2.4 %constant_dynamic-slice_fusion.tiles = bf16[8,4,128,128]{3,2,1,0:T(8,128)(2,1)} fusion(bf16[8,4,512,128]{3,2,1,0:T(8,128)(2,1)} %foot_ref.3, s32[]{:T(128)S(6)} %select_n.11), kind=kLoop, calls=%fused_computation.7 | loop fusion | bytes 2097156 | tf_op jit(solution)/shard_map/dynamic_slice | solution.py:451
  174.9 30.8 %spread_footprints.1 = bf16[8,4,128,128]{3,2,1,0:T(8,128)(2,1)} custom-call(bf16[8,4,512,128]{3,2,1,0:T(8,128)(2,1)} %get-tuple-element.12.grad, f32[8,4,128]{2,1,0:T(4,128)} %get-tuple-element.13.power, bf16[8,4,128,128]{3,2,1,0:T(8,128)(2,1)} %constant_dynamic-slice_fusion.tiles, f32[8,4,128]{2,1,0:T(4,128)} %fusion.live), custom_call_target="tpu_custom_call" | custom-call | tf_op jit(solution)/shard_map/spread_footprints/pallas_call | solution.py:419
  205.8 0.0 copy-done.2
  205.8 0.8 copy.12
  206.6 2.3 %copy.13 = bf16[8,4,128,128]{3,2,1,0:T(8,128)(2,1)} copy(bf16[8,4,128,128]{3,2,1,0:T(8,128)(2,1)} %spread_footprints.1) | data formatting | bytes 2097152
  (2 shorter events, 0.0 us)
Async XLA Ops:
  0.6 0.7 copy-start
  50.1 16.0 %copy-start.1 = (s32[64]{0:T(128)S(1)}, s32[64]{0:T(128)}, u32[]{:S(2)}) copy-start(s32[64]{0:T(128)} %counts_ref.1) | copy-start | bytes 772
  156.1 14.9 %copy-start.3 = (s32[8,4]{1,0:T(8,128)S(1)}, s32[8,4]{1,0:T(8,128)}, u32[]{:S(2)}) copy-start(s32[8,4]{1,0:T(8,128)} %copy.9.block_ref) | copy-start | bytes 388
  172.5 33.2 %copy-start.2 = (bf16[8,128,256]{2,1,0:T(8,128)(2,1)S(1)}, bf16[8,128,256]{2,1,0:T(8,128)(2,1)}, u32[]{:S(2)}) copy-start(bf16[8,128,256]{2,1,0:T(8,128)(2,1)} %get-tuple-element.16) | copy-start | bytes 1572868
